TPU v7x, 256 devices: a whole 4x4x8 slice. The times are simulated.
256 devices in a mesh: row: 16 (over z, core), col: 16 (over x, y).
Axes of the slice: x: 4, y: 4, z: 8, core: 2. Of those that a mesh axis runs over, the one named last changes fastest.
Arguments:
- tiles: float32 [16, 16, 16, 128, 128], P('row', 'col'), may hold values from -1 to 1
- tile_rows: int32 [16, 16, 16], P('row', 'col'), may hold values from 0 to 63, as said below
- tile_cols: int32 [16, 16, 16], P('row', 'col'), may hold values from 0 to 63
- tile_counts: int32 [16, 16], P('row', 'col'), may hold values from 2 to 16, as said below
- objective: float32 [131072], P('col'), may hold values from -6 to 6
- upper: float32 [131072], P('col'), may hold values from 0.2 to 2
- bound_codes: int32 [131072], P('col'), may hold values from 0 to 2
- rhs: float32 [131072], P('row'), may hold values from -6 to 6
- row_codes: int32 [131072], P('row'), may hold values from 0 to 1
Outputs:
- primal: float32 [131072], P('col')
- dual: float32 [131072], P('row')
Inputs may be any that keep to these rules, and one draw needn't show every extreme that they name: `tile_rows`: one device's live slots hold distinct (tile row, tile column) pairs. `tile_counts`: slots at or past a device's count are not part of K; some device has all 16 slots live.
All inputs are finite; a program needn't handle non-finite values. Where the computation divides by a largest or mean magnitude, that divisor is 1e-20 or more.
Results may differ from a plain program's by a relative error of at most 0.00018.
Values sent between devices are 32-bit elements; how exact they have to be, the bound alone decides.
A program may use at most 64 MiB of HBM per device.

v0:
```python
import jax
import jax.numpy as jnp
from jax import lax
from jax.sharding import PartitionSpec as P

TILE_BLOCK = 16
TILE_ROWS = 64
TILE_COLS = 64
OUTER = 2
INNER = 4


def project_primal(values, bound_codes, upper):
    values = jnp.where(bound_codes >= 1, jnp.maximum(values, 0.0), values)
    return jnp.where(bound_codes == 2, jnp.minimum(values, upper), values)


def project_dual(values, row_codes):
    return jnp.where(row_codes == 1, jnp.maximum(values, 0.0), values)


def step_update(step_size, weight, inter_term, primal_sq, dual_sq, counter):
    shrink = 1.0 - (counter + 1) ** (-0.3)
    growth = 1.0 + (counter + 1) ** (-0.6)
    numer = shrink * (weight * primal_sq + dual_sq / weight + 1e-06)
    return numer / jnp.maximum(2.0 * jnp.abs(inter_term), numer / (growth * step_size))


def tile_products(tile_data, row_slots, col_slots, live_count, vector, direction):
    highest = lax.Precision.HIGHEST
    width = tile_data.shape[-1]
    groups = (live_count + TILE_BLOCK - 1) // TILE_BLOCK
    if direction == "forward":
        shaped = vector.reshape(TILE_COLS, width)
        out_rows = TILE_ROWS
    else:
        shaped = vector.reshape(TILE_ROWS, width)
        out_rows = TILE_COLS

    def visit(group, total):
        first_slot = group * TILE_BLOCK
        alive = (first_slot + jnp.arange(TILE_BLOCK, dtype=jnp.int32) < live_count).astype(
            jnp.float32
        )
        row_hot = (row_slots[:, None] == jnp.arange(TILE_ROWS, dtype=jnp.int32)[None, :]).astype(
            jnp.float32
        )
        col_hot = (col_slots[:, None] == jnp.arange(TILE_COLS, dtype=jnp.int32)[None, :]).astype(
            jnp.float32
        )
        if direction == "forward":
            pieces = jnp.dot(col_hot, shaped, precision=highest)
            images = jnp.einsum("tij,tj->ti", tile_data, pieces, precision=highest)
            return total + jnp.einsum(
                "tk,ti->ki", row_hot * alive[:, None], images, precision=highest
            )
        else:
            pieces = jnp.dot(row_hot, shaped, precision=highest)
            images = jnp.einsum("tij,ti->tj", tile_data, pieces, precision=highest)
            return total + jnp.einsum(
                "tk,tj->kj", col_hot * alive[:, None], images, precision=highest
            )

    total = lax.fori_loop(0, groups, visit, jnp.zeros((out_rows, width), jnp.float32))
    return total.reshape(-1)


def per_device(
    tiles, tile_rows, tile_cols, tile_counts, objective, upper, bound_codes, rhs, row_codes
):
    tile_data = tiles[0, 0]
    row_slots = tile_rows[0, 0]
    col_slots = tile_cols[0, 0]
    live_count = tile_counts[0, 0]
    row_place = lax.axis_index("row")
    col_place = lax.axis_index("col")
    primal_mask = (row_place == 0).astype(jnp.float32)
    dual_mask = (col_place == 0).astype(jnp.float32)

    def forward(vector):
        partial_rows = tile_products(tile_data, row_slots, col_slots, live_count, vector, "forward")
        return lax.psum(partial_rows, "col")

    def backward(vector):
        partial_cols = tile_products(
            tile_data, row_slots, col_slots, live_count, vector, "backward"
        )
        return lax.psum(partial_cols, "row")

    def pair_sums(primal_term, dual_term):
        return lax.psum((primal_term * primal_mask, dual_term * dual_mask), ("row", "col"))

    alive_slots = (jnp.arange(tile_data.shape[0], dtype=jnp.int32) < live_count).astype(jnp.float32)
    local_largest = jnp.max(jnp.abs(tile_data) * alive_slots[:, None, None])
    largest = lax.pmax(local_largest, ("row", "col"))
    step_size = 0.05 / (largest + 1e-06)
    object_sq, rhs_sq = pair_sums(jnp.sum(objective * objective), jnp.sum(rhs * rhs))
    weight = jnp.sqrt((object_sq + 1e-06) / (rhs_sq + 1e-06))
    primal = jnp.zeros_like(objective)
    dual_piece = jnp.zeros_like(rhs)
    row_image = jnp.zeros_like(rhs)
    col_image = jnp.zeros_like(objective)
    counter = 0
    for cycle_index in range(OUTER):
        start_primal = primal
        start_dual = dual_piece
        primal_total = jnp.zeros_like(objective)
        dual_total = jnp.zeros_like(rhs)
        weight_total = jnp.zeros((), jnp.float32)
        for step_index in range(INNER):
            counter += 1
            next_primal = project_primal(
                primal - step_size / weight * (objective - col_image), bound_codes, upper
            )
            next_row = forward(next_primal)
            next_dual = project_dual(
                dual_piece + step_size * weight * (rhs - (2.0 * next_row - row_image)), row_codes
            )
            next_col = backward(next_dual)
            primal_move = next_primal - primal
            dual_move = next_dual - dual_piece
            inter_term, primal_sq, dual_sq = lax.psum(
                (
                    jnp.sum(primal_move * (next_col - col_image)) * primal_mask,
                    jnp.sum(primal_move * primal_move) * primal_mask,
                    jnp.sum(dual_move * dual_move) * dual_mask,
                ),
                ("row", "col"),
            )
            primal_total = primal_total + step_size * next_primal
            dual_total = dual_total + step_size * next_dual
            weight_total = weight_total + step_size
            step_size = step_update(step_size, weight, inter_term, primal_sq, dual_sq, counter)
            primal, dual_piece, row_image, col_image = (next_primal, next_dual, next_row, next_col)
        primal = primal_total / weight_total
        dual_piece = dual_total / weight_total
        primal_shift = primal - start_primal
        dual_shift = dual_piece - start_dual
        primal_drift, dual_drift = pair_sums(
            jnp.sum(primal_shift * primal_shift), jnp.sum(dual_shift * dual_shift)
        )
        weight = jnp.sqrt(weight * jnp.sqrt(dual_drift + 1e-06) / jnp.sqrt(primal_drift + 1e-06))
        if cycle_index + 1 < OUTER:
            row_image = forward(primal)
            col_image = backward(dual_piece)
    return (primal, dual_piece)


def solution(mesh):
    placed = (
        P("row", "col", None, None, None),
        P("row", "col", None),
        P("row", "col", None),
        P("row", "col"),
        P("col"),
        P("col"),
        P("col"),
        P("row"),
        P("row"),
    )
    return jax.shard_map(
        per_device, mesh=mesh, in_specs=placed, out_specs=(P("col"), P("row")), check_vma=False
    )
```

profile of v0, /device:TPU:32, one launch (start us, length us, event | category | flops | bytes accessed | tf_op | source)
XLA Modules:
  0.0 1723.5 jit_solution(5136370811758483441)
XLA Ops:
  10.5 79.8 %all-reduce.7 = (f32[]{:T(128)}, f32[]{:T(128)}) all-reduce(f32[]{:T(128)S(6)} %mul.700, f32[]{:T(128)S(6)} %mul.702), channel_id=1, replica_groups=mesh['row'=16,'col'=16] {'row','col'}, use_global_device_ids=true, to_apply=%region_1.0 | all-reduce | flops 2 | bytes 16 | tf_op jit(solution)/shard_map/psum | solution.py:91
  91.7 2.2 fusion.120
  93.9 73.6 %pmax.7 = f32[]{:T(128)} all-reduce(f32[]{:T(128)} %fusion.120), channel_id=1, replica_groups=mesh['row'=16,'col'=16] {'row','col'}, use_global_device_ids=true, to_apply=%region_5.0 | all-reduce | flops 1 | bytes 8 | tf_op jit(solution)/shard_map/pmax | solution.py:95
  169.1 1.7 fusion.117
  172.5 70.9 %psum.297 = f32[8192]{0:T(1024)S(1)} all-reduce(f32[8192]{0:T(1024)S(1)} %bitcast.318), channel_id=1, replica_groups=mesh['row'=16,'col'=16] {'col'}, use_global_device_ids=true, to_apply=%region_10.11 | all-reduce | flops 8192 | bytes 65536 | tf_op jit(solution)/shard_map/psum | solution.py:82
  244.2 1.0 fusion.115
  246.2 42.2 %psum.299 = f32[8192]{0:T(1024)S(1)} all-reduce(f32[8192]{0:T(1024)S(1)} %bitcast.319), channel_id=1, replica_groups=mesh['row'=16,'col'=16] {'row'}, use_global_device_ids=true, to_apply=%region_15.16 | all-reduce | flops 8192 | bytes 65536 | tf_op jit(solution)/shard_map/psum | solution.py:88
  291.1 74.6 %all-reduce.6 = (f32[]{:T(128)}, f32[]{:T(128)}, f32[]{:T(128)}) all-reduce(f32[]{:T(128)S(6)} %mul.708, f32[]{:T(128)S(6)} %mul.715, f32[]{:T(128)S(6)} %mul.717), channel_id=1, replica_groups=mesh['row'=16,'col'=16] {'row','col'}, use_global_device_ids=true, to_apply=%region_7.8 | all-reduce | flops 3 | bytes 24 | tf_op jit(solution)/shard_map/psum | solution.py:122
  367.9 1.7 fusion.113
  369.6 1.0 while.206
  370.6 71.0 %psum.302 = f32[8192]{0:T(1024)S(1)} all-reduce(f32[8192]{0:T(1024)S(1)} %bitcast.320), channel_id=1, replica_groups=mesh['row'=16,'col'=16] {'col'}, use_global_device_ids=true, to_apply=%region_22.23 | all-reduce | flops 8192 | bytes 65536 | tf_op jit(solution)/shard_map/psum | solution.py:82
  442.4 1.0 fusion.111
  444.4 42.2 %psum.304 = f32[8192]{0:T(1024)S(1)} all-reduce(f32[8192]{0:T(1024)S(1)} %bitcast.321), channel_id=1, replica_groups=mesh['row'=16,'col'=16] {'row'}, use_global_device_ids=true, to_apply=%region_27.28 | all-reduce | flops 8192 | bytes 65536 | tf_op jit(solution)/shard_map/psum | solution.py:88
  489.3 74.6 %all-reduce.5 = (f32[]{:T(128)}, f32[]{:T(128)}, f32[]{:T(128)}) all-reduce(f32[]{:T(128)S(6)} %mul.722, f32[]{:T(128)S(6)} %mul.729, f32[]{:T(128)S(6)} %mul.731), channel_id=1, replica_groups=mesh['row'=16,'col'=16] {'row','col'}, use_global_device_ids=true, to_apply=%region_19.20 | all-reduce | flops 3 | bytes 24 | tf_op jit(solution)/shard_map/psum | solution.py:122
  566.1 1.7 fusion.109
  567.8 1.0 while.208
  568.8 71.0 %psum.307 = f32[8192]{0:T(1024)S(1)} all-reduce(f32[8192]{0:T(1024)S(1)} %bitcast.322), channel_id=1, replica_groups=mesh['row'=16,'col'=16] {'col'}, use_global_device_ids=true, to_apply=%region_34.35 | all-reduce | flops 8192 | bytes 65536 | tf_op jit(solution)/shard_map/psum | solution.py:82
  640.6 1.0 fusion.107
  642.6 42.2 %psum.309 = f32[8192]{0:T(1024)S(1)} all-reduce(f32[8192]{0:T(1024)S(1)} %bitcast.323), channel_id=1, replica_groups=mesh['row'=16,'col'=16] {'row'}, use_global_device_ids=true, to_apply=%region_39.40 | all-reduce | flops 8192 | bytes 65536 | tf_op jit(solution)/shard_map/psum | solution.py:88
  687.5 74.6 %all-reduce.4 = (f32[]{:T(128)}, f32[]{:T(128)}, f32[]{:T(128)}) all-reduce(f32[]{:T(128)S(6)} %mul.736, f32[]{:T(128)S(6)} %mul.743, f32[]{:T(128)S(6)} %mul.745), channel_id=1, replica_groups=mesh['row'=16,'col'=16] {'row','col'}, use_global_device_ids=true, to_apply=%region_31.32 | all-reduce | flops 3 | bytes 24 | tf_op jit(solution)/shard_map/psum | solution.py:122
  765.0 1.7 fusion.105
  767.7 71.0 %psum.312 = f32[8192]{0:T(1024)S(1)} all-reduce(f32[8192]{0:T(1024)S(1)} %bitcast.324), channel_id=1, replica_groups=mesh['row'=16,'col'=16] {'col'}, use_global_device_ids=true, to_apply=%region_46.47 | all-reduce | flops 8192 | bytes 65536 | tf_op jit(solution)/shard_map/psum | solution.py:82
  839.6 1.0 fusion.103
  845.0 1.7 fusion.97
  846.8 1.0 while.214
  850.3 88.5 %all-reduce.15.cloned.1.call-done = (f32[8192]{0:T(1024)}, f32[8192]{0:T(1024)}) async-done(((f32[8192]{0:T(1024)}, f32[8192]{0:T(1024)}), (f32[8192]{0:T(1024)}, f32[8192]{0:T(1024)})) %all-reduce.15.cloned.1.call-update) | async-done | bytes 65552 | tf_op jit(solution)/shard_map/psum | solution.py:88
  938.8 1.4 multiply_reduce_fusion.11
  941.5 77.5 %all-reduce.3 = (f32[]{:T(128)}, f32[]{:T(128)}, f32[]{:T(128)}, f32[]{:T(128)}, f32[]{:T(128)}) all-reduce(f32[]{:T(128)S(6)} %mul.750, f32[]{:T(128)S(6)} %mul.757, f32[]{:T(128)S(6)} %mul.759, f32[]{:T(128)S(6)} %mul.775, f32[]{:T(128)S(6)} %mul.778), channel_id=1, replica_groups=mesh['row'=16,'col'=16] {'row','col'}, use_global_device_ids=true, to_apply=%region_43.44 | all-reduce | flops 5 | bytes 40 | tf_op jit(solution)/shard_map/psum | solution.py:122
  1022.6 1.7 fusion.99
  1026.0 88.5 %all-reduce.13.cloned.1.call-done = (f32[8192]{0:T(1024)}, f32[8192]{0:T(1024)}) async-done(((f32[8192]{0:T(1024)}, f32[8192]{0:T(1024)}), (f32[8192]{0:T(1024)}, f32[8192]{0:T(1024)})) %all-reduce.13.cloned.1.call-update) | async-done | bytes 65552 | tf_op jit(solution)/shard_map/psum | solution.py:82
  1114.5 1.4 multiply_reduce_fusion.7
  1116.1 1.0 fusion.95
  1118.1 43.5 %psum.323 = f32[8192]{0:T(1024)S(1)} all-reduce(f32[8192]{0:T(1024)S(1)} %bitcast.329), channel_id=1, replica_groups=mesh['row'=16,'col'=16] {'row'}, use_global_device_ids=true, to_apply=%region_73.74 | all-reduce | flops 8192 | bytes 65536 | tf_op jit(solution)/shard_map/psum | solution.py:88
  1164.2 77.8 %all-reduce.2 = (f32[]{:T(128)}, f32[]{:T(128)}, f32[]{:T(128)}) all-reduce(f32[]{:T(128)S(6)} %mul.783, f32[]{:T(128)S(6)} %mul.790, f32[]{:T(128)S(6)} %mul.792), channel_id=1, replica_groups=mesh['row'=16,'col'=16] {'row','col'}, use_global_device_ids=true, to_apply=%region_62.63 | all-reduce | flops 3 | bytes 24 | tf_op jit(solution)/shard_map/psum | solution.py:122
  1244.4 1.7 fusion.93
  1246.1 1.0 while.216
  1247.1 70.4 %psum.326 = f32[8192]{0:T(1024)S(1)} all-reduce(f32[8192]{0:T(1024)S(1)} %bitcast.330), channel_id=1, replica_groups=mesh['row'=16,'col'=16] {'col'}, use_global_device_ids=true, to_apply=%region_80.81 | all-reduce | flops 8192 | bytes 65536 | tf_op jit(solution)/shard_map/psum | solution.py:82
  1318.3 1.0 fusion.91
  1320.3 42.5 %psum.328 = f32[8192]{0:T(1024)S(1)} all-reduce(f32[8192]{0:T(1024)S(1)} %bitcast.331), channel_id=1, replica_groups=mesh['row'=16,'col'=16] {'row'}, use_global_device_ids=true, to_apply=%region_85.86 | all-reduce | flops 8192 | bytes 65536 | tf_op jit(solution)/shard_map/psum | solution.py:88
  1365.5 74.6 %all-reduce.1 = (f32[]{:T(128)}, f32[]{:T(128)}, f32[]{:T(128)}) all-reduce(f32[]{:T(128)S(6)} %mul.799, f32[]{:T(128)S(6)} %mul.806, f32[]{:T(128)S(6)} %mul.808), channel_id=1, replica_groups=mesh['row'=16,'col'=16] {'row','col'}, use_global_device_ids=true, to_apply=%region_77.78 | all-reduce | flops 3 | bytes 24 | tf_op jit(solution)/shard_map/psum | solution.py:122
  1442.4 1.7 fusion.89
  1444.2 1.0 while.218
  1445.2 71.0 %psum.331 = f32[8192]{0:T(1024)S(1)} all-reduce(f32[8192]{0:T(1024)S(1)} %bitcast.332), channel_id=1, replica_groups=mesh['row'=16,'col'=16] {'col'}, use_global_device_ids=true, to_apply=%region_92.93 | all-reduce | flops 8192 | bytes 65536 | tf_op jit(solution)/shard_map/psum | solution.py:82
  1516.9 1.0 fusion.87
  1518.9 43.1 %psum.333 = f32[8192]{0:T(1024)S(1)} all-reduce(f32[8192]{0:T(1024)S(1)} %bitcast.333), channel_id=1, replica_groups=mesh['row'=16,'col'=16] {'row'}, use_global_device_ids=true, to_apply=%region_97.98 | all-reduce | flops 8192 | bytes 65536 | tf_op jit(solution)/shard_map/psum | solution.py:88
  1564.7 74.6 %all-reduce = (f32[]{:T(128)}, f32[]{:T(128)}, f32[]{:T(128)}) all-reduce(f32[]{:T(128)S(6)} %mul.815, f32[]{:T(128)S(6)} %mul.822, f32[]{:T(128)S(6)} %mul.824), channel_id=1, replica_groups=mesh['row'=16,'col'=16] {'row','col'}, use_global_device_ids=true, to_apply=%region_89.90 | all-reduce | flops 3 | bytes 24 | tf_op jit(solution)/shard_map/psum | solution.py:122
  1642.3 1.7 fusion.85
  1645.0 71.0 %psum.335 = f32[8192]{0:T(1024)S(1)} all-reduce(f32[8192]{0:T(1024)S(1)} %bitcast.317), channel_id=1, replica_groups=mesh['row'=16,'col'=16] {'col'}, use_global_device_ids=true, to_apply=%region_102.103 | all-reduce | flops 8192 | bytes 65536 | tf_op jit(solution)/shard_map/psum | solution.py:82
  (138 shorter events, 47.2 us)
Async XLA Ops:
  7.2 0.8 copy-start.1
  7.2 1.4 copy-start.2
  7.2 161.9 %copy-start = (f32[1,1,16,128,128]{4,3,2,1,0:T(8,128)S(1)}, f32[1,1,16,128,128]{4,3,2,1,0:T(8,128)}, u32[]{:S(2)}) copy-start(f32[1,1,16,128,128]{4,3,2,1,0:T(8,128)} %param.43) | copy-start | bytes 3145732
  7.2 931.6 %all-reduce.15.cloned.1.call-start = ((), (), s32[]{:S(2)}) async-start(), calls=%async_computation.1 | async-start | bytes 131072 | tf_op jit(solution)/shard_map/psum | solution.py:88
  91.7 76.6 %copy-start.3 = (f32[8192]{0:T(1024)S(1)}, f32[8192]{0:T(1024)}, u32[]{:S(2)}) copy-start(f32[8192]{0:T(1024)} %param.48) | copy-start | bytes 98308
  91.7 76.6 %copy-start.11 = (s32[8192]{0:T(1024)S(1)}, s32[8192]{0:T(1024)}, u32[]{:S(2)}) copy-start(s32[8192]{0:T(1024)} %param.49) | copy-start | bytes 98308
  168.3 0.7 copy-start.12
  170.9 0.7 copy-start.13
  172.5 70.9 %copy-start.10 = (s32[8192]{0:T(1024)S(1)}, s32[8192]{0:T(1024)}, u32[]{:S(2)}) copy-start(s32[8192]{0:T(1024)} %param.51) | copy-start | bytes 98308
  841.6 0.6 copy-start.4
  844.1 0.6 copy-start.5
  844.8 269.7 %all-reduce.13.cloned.1.call-start = ((), (), s32[]{:S(2)}) async-start(), calls=%async_computation | async-start | bytes 131072 | tf_op jit(solution)/shard_map/psum | solution.py:82
  847.8 0.6 copy-start.6
  940.2 82.1 %copy-start.8 = (f32[8192]{0:T(1024)S(1)}, f32[8192]{0:T(1024)}, u32[]{:S(2)}) copy-start(f32[8192]{0:T(1024)} %get-tuple-element.1828) | copy-start | bytes 98308
  1025.3 0.6 copy-start.7
  1247.1 70.4 %copy-start.9 = (f32[8192]{0:T(1024)S(1)}, f32[8192]{0:T(1024)}, u32[]{:S(2)}) copy-start(f32[8192]{0:T(1024)} %get-tuple-element.1827) | copy-start | bytes 98308
Sparse Core Ops, SparseCore 0:
  844.9 93.8 all-reduce.14
  1026.1 88.3 all-reduce.12
where the time goes:
time: 1730 us; the launch traced here: 1720 us
  blocking collectives  1430 us (83%)
  waiting for transfers between devices  177 us (10%)
  between operations  49.5 us (3%)
  matrix products  31.9 us (2%)
  other arithmetic  28 us (2%)
    psum x7, blocking collectives, per_device(): lax.psum((jnp.sum(primal_move * (next_col - col_image)) * primal_mask, jn...  528 us
    psum x7, blocking collectives, forward(): return lax.psum(partial_rows, 'col')  496 us
    psum x6, blocking collectives, backward(): return lax.psum(partial_cols, 'row')  256 us
    psum x1, waiting for transfers between devices, backward(): return lax.psum(partial_cols, 'row')  88.5 us
    psum x1, waiting for transfers between devices, forward(): return lax.psum(partial_rows, 'col')  88.5 us
    psum x1, blocking collectives, pair_sums(): lax.psum((primal_term * primal_mask, dual_term * dual_mask), ('row', 'col'))  79.8 us
    pmax x1, blocking collectives, per_device(): largest = lax.pmax(local_largest, ('row', 'col'))  73.6 us
  transfers between devices with their start and end apart: 2, of which 2 were waited for; matrix products, arithmetic and copies ran while one was open for 0% of the time, Pallas kernels for 0%

commit v1 on v0

--- a/solution.py
+++ b/solution.py
@@ -119,13 +119,13 @@
             next_col = backward(next_dual)
             primal_move = next_primal - primal
             dual_move = next_dual - dual_piece
-            inter_term, primal_sq, dual_sq = lax.psum(
+            choose_strips_all_on_mesh = lambda slab_in: lax.psum(lax.psum(slab_in, "row"), "col")
+            inter_term, primal_sq, dual_sq = choose_strips_all_on_mesh(
                 (
                     jnp.sum(primal_move * (next_col - col_image)) * primal_mask,
                     jnp.sum(primal_move * primal_move) * primal_mask,
                     jnp.sum(dual_move * dual_move) * dual_mask,
-                ),
-                ("row", "col"),
+                )
             )
             primal_total = primal_total + step_size * next_primal
             dual_total = dual_total + step_size * next_dual

time: 1730 us -> 1690 us (0.977)
  waiting for transfers between devices: 177 us -> 87.1 us
  blocking collectives: 1430 us -> 1490 us
    psum x7 -> x13, blocking collectives: 528 us -> 400 us  [the longest x7 256 us: per_device(): lax.psum(lax.psum(slab_in, 'row'), 'col')]
    psum x6 -> x8, blocking collectives: 256 us -> 360 us  [backward(): return lax.psum(partial_cols, 'row')]
    psum x1 -> x0, waiting for transfers between devices: 88.5 us -> none  [backward(): return lax.psum(partial_cols, 'row')]
    psum x1 -> x2, blocking collectives: 79.8 us -> 157 us  [pair_sums(): lax.psum((primal_term * primal_mask, dual_term * dual_mask), ('row', 'col'))]
  transfers between devices with their start and end apart: 2 -> 1, of which waited for: 2 -> 1; matrix products, arithmetic and copies ran while one was open for 0% -> 0% of each run, Pallas kernels for 0% -> 0%
where the time goes in v1:
time: 1690 us
  blocking collectives  1490 us (88%)
  waiting for transfers between devices  87.1 us (5%)
  between operations  49.2 us (3%)
  matrix products  31.9 us (2%)
  other arithmetic  27.2 us (2%)
    psum x7, blocking collectives, forward(): return lax.psum(partial_rows, 'col')  498 us
    psum x8, blocking collectives, backward(): return lax.psum(partial_cols, 'row')  360 us
    psum x7, blocking collectives, per_device(): lax.psum(lax.psum(slab_in, 'row'), 'col')  256 us
    psum x2, blocking collectives, pair_sums(): lax.psum((primal_term * primal_mask, dual_term * dual_mask), ('row', 'col'))  157 us
    psum x6, blocking collectives, per_device(): lax.psum(slab_in, 'row')  145 us
    psum x1, waiting for transfers between devices, forward(): return lax.psum(partial_rows, 'col')  87.1 us
    pmax x1, blocking collectives, per_device(): largest = lax.pmax(local_largest, ('row', 'col'))  73.6 us
  transfers between devices with their start and end apart: 1, of which 1 were waited for; matrix products, arithmetic and copies ran while one was open for 0% of the time, Pallas kernels for 0%

profile of v1, /device:TPU:32, one launch (start us, length us, event | category | flops | bytes accessed | tf_op | source)
XLA Modules:
  0.0 1686.9 jit_solution(3763424420883263469)
XLA Ops:
  10.5 79.8 %all-reduce.1 = (f32[]{:T(128)}, f32[]{:T(128)}) all-reduce(f32[]{:T(128)S(6)} %mul.700, f32[]{:T(128)S(6)} %mul.702), channel_id=1, replica_groups=mesh['row'=16,'col'=16] {'row','col'}, use_global_device_ids=true, to_apply=%region_1.0 | all-reduce | flops 2 | bytes 16 | tf_op jit(solution)/shard_map/psum | solution.py:91
  91.7 2.2 fusion.120
  93.9 73.6 %pmax.7 = f32[]{:T(128)} all-reduce(f32[]{:T(128)} %fusion.120), channel_id=1, replica_groups=mesh['row'=16,'col'=16] {'row','col'}, use_global_device_ids=true, to_apply=%region_5.0 | all-reduce | flops 1 | bytes 8 | tf_op jit(solution)/shard_map/pmax | solution.py:95
  169.1 1.7 fusion.117
  172.5 70.9 %psum.445 = f32[8192]{0:T(1024)S(1)} all-reduce(f32[8192]{0:T(1024)S(1)} %bitcast.318), channel_id=1, replica_groups=mesh['row'=16,'col'=16] {'col'}, use_global_device_ids=true, to_apply=%region_11.12 | all-reduce | flops 8192 | bytes 65536 | tf_op jit(solution)/shard_map/psum | solution.py:82
  244.2 1.0 fusion.115
  246.2 42.2 %psum.448 = f32[8192]{0:T(1024)S(1)} all-reduce(f32[8192]{0:T(1024)S(1)} %bitcast.319), channel_id=1, replica_groups=mesh['row'=16,'col'=16] {'row'}, use_global_device_ids=true, to_apply=%region_17.18 | all-reduce | flops 8192 | bytes 65536 | tf_op jit(solution)/shard_map/psum | solution.py:88
  291.1 24.1 %all-reduce.16 = (f32[]{:T(128)}, f32[]{:T(128)}, f32[]{:T(128)}) all-reduce(f32[]{:T(128)S(6)} %mul.708, f32[]{:T(128)S(6)} %mul.715, f32[]{:T(128)S(6)} %mul.717), channel_id=1, replica_groups=mesh['row'=16,'col'=16] {'row'}, use_global_device_ids=true, to_apply=%region_7.8 | all-reduce | flops 3 | bytes 24 | tf_op jit(solution)/shard_map/psum | solution.py:122
  315.2 36.1 %all-reduce.9 = (f32[]{:T(128)}, f32[]{:T(128)}, f32[]{:T(128)}) all-reduce(f32[]{:T(128)} %get-tuple-element.1847, f32[]{:T(128)} %get-tuple-element.1848, f32[]{:T(128)} %get-tuple-element.1849), channel_id=1, replica_groups=mesh['row'=16,'col'=16] {'col'}, use_global_device_ids=true, to_apply=%region_8.9 | all-reduce | flops 3 | bytes 24 | tf_op jit(solution)/shard_map/psum | solution.py:122
  353.6 1.7 fusion.113
  356.3 71.4 %psum.453 = f32[8192]{0:T(1024)S(1)} all-reduce(f32[8192]{0:T(1024)S(1)} %bitcast.320), channel_id=1, replica_groups=mesh['row'=16,'col'=16] {'col'}, use_global_device_ids=true, to_apply=%region_26.27 | all-reduce | flops 8192 | bytes 65536 | tf_op jit(solution)/shard_map/psum | solution.py:82
  428.5 1.0 fusion.111
  430.5 45.7 %psum.456 = f32[8192]{0:T(1024)S(1)} all-reduce(f32[8192]{0:T(1024)S(1)} %bitcast.321), channel_id=1, replica_groups=mesh['row'=16,'col'=16] {'row'}, use_global_device_ids=true, to_apply=%region_32.33 | all-reduce | flops 8192 | bytes 65536 | tf_op jit(solution)/shard_map/psum | solution.py:88
  478.9 24.1 %all-reduce.15 = (f32[]{:T(128)}, f32[]{:T(128)}, f32[]{:T(128)}) all-reduce(f32[]{:T(128)S(6)} %mul.722, f32[]{:T(128)S(6)} %mul.729, f32[]{:T(128)S(6)} %mul.731), channel_id=1, replica_groups=mesh['row'=16,'col'=16] {'row'}, use_global_device_ids=true, to_apply=%region_22.23 | all-reduce | flops 3 | bytes 24 | tf_op jit(solution)/shard_map/psum | solution.py:122
  503.0 36.1 %all-reduce.8 = (f32[]{:T(128)}, f32[]{:T(128)}, f32[]{:T(128)}) all-reduce(f32[]{:T(128)} %get-tuple-element.1844, f32[]{:T(128)} %get-tuple-element.1845, f32[]{:T(128)} %get-tuple-element.1846), channel_id=1, replica_groups=mesh['row'=16,'col'=16] {'col'}, use_global_device_ids=true, to_apply=%region_23.24 | all-reduce | flops 3 | bytes 24 | tf_op jit(solution)/shard_map/psum | solution.py:122
  541.4 1.7 fusion.109
  544.1 71.4 %psum.461 = f32[8192]{0:T(1024)S(1)} all-reduce(f32[8192]{0:T(1024)S(1)} %bitcast.322), channel_id=1, replica_groups=mesh['row'=16,'col'=16] {'col'}, use_global_device_ids=true, to_apply=%region_41.42 | all-reduce | flops 8192 | bytes 65536 | tf_op jit(solution)/shard_map/psum | solution.py:82
  616.4 1.0 fusion.107
  618.3 45.7 %psum.464 = f32[8192]{0:T(1024)S(1)} all-reduce(f32[8192]{0:T(1024)S(1)} %bitcast.323), channel_id=1, replica_groups=mesh['row'=16,'col'=16] {'row'}, use_global_device_ids=true, to_apply=%region_47.48 | all-reduce | flops 8192 | bytes 65536 | tf_op jit(solution)/shard_map/psum | solution.py:88
  666.7 24.1 %all-reduce.14 = (f32[]{:T(128)}, f32[]{:T(128)}, f32[]{:T(128)}) all-reduce(f32[]{:T(128)S(6)} %mul.736, f32[]{:T(128)S(6)} %mul.743, f32[]{:T(128)S(6)} %mul.745), channel_id=1, replica_groups=mesh['row'=16,'col'=16] {'row'}, use_global_device_ids=true, to_apply=%region_37.38 | all-reduce | flops 3 | bytes 24 | tf_op jit(solution)/shard_map/psum | solution.py:122
  690.9 36.3 %all-reduce.7 = (f32[]{:T(128)}, f32[]{:T(128)}, f32[]{:T(128)}) all-reduce(f32[]{:T(128)} %get-tuple-element.1841, f32[]{:T(128)} %get-tuple-element.1842, f32[]{:T(128)} %get-tuple-element.1843), channel_id=1, replica_groups=mesh['row'=16,'col'=16] {'col'}, use_global_device_ids=true, to_apply=%region_38.39 | all-reduce | flops 3 | bytes 24 | tf_op jit(solution)/shard_map/psum | solution.py:122
  729.9 1.7 fusion.105
  732.7 71.4 %psum.469 = f32[8192]{0:T(1024)S(1)} all-reduce(f32[8192]{0:T(1024)S(1)} %bitcast.324), channel_id=1, replica_groups=mesh['row'=16,'col'=16] {'col'}, use_global_device_ids=true, to_apply=%region_56.57 | all-reduce | flops 8192 | bytes 65536 | tf_op jit(solution)/shard_map/psum | solution.py:82
  807.6 45.7 %psum.472 = f32[8192]{0:T(1024)S(1)} all-reduce(f32[8192]{0:T(1024)S(1)} %bitcast.325), channel_id=1, replica_groups=mesh['row'=16,'col'=16] {'row'}, use_global_device_ids=true, to_apply=%region_62.63 | all-reduce | flops 8192 | bytes 65536 | tf_op jit(solution)/shard_map/psum | solution.py:88
  854.2 1.0 fusion.101
  858.0 45.8 %all-reduce.13 = (f32[8192]{0:T(1024)S(1)}, f32[]{:T(128)}, f32[]{:T(128)}, f32[]{:T(128)}) all-reduce(f32[8192]{0:T(1024)S(1)} %bitcast.326, f32[]{:T(128)S(6)} %mul.750, f32[]{:T(128)S(6)} %mul.757, f32[]{:T(128)S(6)} %mul.759), channel_id=1, replica_groups=mesh['row'=16,'col'=16] {'row'}, use_global_device_ids=true, to_apply=%region_72.73 | all-reduce | flops 8195 | bytes 65560 | tf_op jit(solution)/shard_map/psum | solution.py:88
  903.8 36.2 %all-reduce.6 = (f32[]{:T(128)}, f32[]{:T(128)}, f32[]{:T(128)}) all-reduce(f32[]{:T(128)} %get-tuple-element.1838, f32[]{:T(128)} %get-tuple-element.1839, f32[]{:T(128)} %get-tuple-element.1840), channel_id=1, replica_groups=mesh['row'=16,'col'=16] {'col'}, use_global_device_ids=true, to_apply=%region_53.54 | all-reduce | flops 3 | bytes 24 | tf_op jit(solution)/shard_map/psum | solution.py:122
  943.1 77.5 %all-reduce = (f32[]{:T(128)}, f32[]{:T(128)}) all-reduce(f32[]{:T(128)S(6)} %mul.775, f32[]{:T(128)S(6)} %mul.778), channel_id=1, replica_groups=mesh['row'=16,'col'=16] {'row','col'}, use_global_device_ids=true, to_apply=%region_67.68 | all-reduce | flops 2 | bytes 16 | tf_op jit(solution)/shard_map/psum | solution.py:91
  1022.5 1.7 fusion.99
  1025.3 1.7 fusion.97
  1027.0 1.0 while.214
  1028.7 87.1 %all-reduce.19.cloned.1.call-done = (f32[8192]{0:T(1024)}, f32[8192]{0:T(1024)}) async-done(((f32[8192]{0:T(1024)}, f32[8192]{0:T(1024)}), (f32[8192]{0:T(1024)}, f32[8192]{0:T(1024)})) %all-reduce.19.cloned.1.call-update) | async-done | bytes 65552 | tf_op jit(solution)/shard_map/psum | solution.py:82
  1115.8 1.4 multiply_reduce_fusion.7
  1119.4 43.5 %psum.484 = f32[8192]{0:T(1024)S(1)} all-reduce(f32[8192]{0:T(1024)S(1)} %bitcast.329), channel_id=1, replica_groups=mesh['row'=16,'col'=16] {'row'}, use_global_device_ids=true, to_apply=%region_87.88 | all-reduce | flops 8192 | bytes 65536 | tf_op jit(solution)/shard_map/psum | solution.py:88
  1165.4 24.1 %all-reduce.12 = (f32[]{:T(128)}, f32[]{:T(128)}, f32[]{:T(128)}) all-reduce(f32[]{:T(128)S(6)} %mul.783, f32[]{:T(128)S(6)} %mul.790, f32[]{:T(128)S(6)} %mul.792), channel_id=1, replica_groups=mesh['row'=16,'col'=16] {'row'}, use_global_device_ids=true, to_apply=%region_74.75 | all-reduce | flops 3 | bytes 24 | tf_op jit(solution)/shard_map/psum | solution.py:122
  1189.5 39.0 %all-reduce.4 = (f32[]{:T(128)}, f32[]{:T(128)}, f32[]{:T(128)}) all-reduce(f32[]{:T(128)} %get-tuple-element.1834, f32[]{:T(128)} %get-tuple-element.1835, f32[]{:T(128)} %get-tuple-element.1836), channel_id=1, replica_groups=mesh['row'=16,'col'=16] {'col'}, use_global_device_ids=true, to_apply=%region_75.76 | all-reduce | flops 3 | bytes 24 | tf_op jit(solution)/shard_map/psum | solution.py:122
  1230.7 1.7 fusion.93
  1233.5 69.8 %psum.489 = f32[8192]{0:T(1024)S(1)} all-reduce(f32[8192]{0:T(1024)S(1)} %bitcast.330), channel_id=1, replica_groups=mesh['row'=16,'col'=16] {'col'}, use_global_device_ids=true, to_apply=%region_96.97 | all-reduce | flops 8192 | bytes 65536 | tf_op jit(solution)/shard_map/psum | solution.py:82
  1306.0 45.7 %psum.492 = f32[8192]{0:T(1024)S(1)} all-reduce(f32[8192]{0:T(1024)S(1)} %bitcast.331), channel_id=1, replica_groups=mesh['row'=16,'col'=16] {'row'}, use_global_device_ids=true, to_apply=%region_102.103 | all-reduce | flops 8192 | bytes 65536 | tf_op jit(solution)/shard_map/psum | solution.py:88
  1354.4 24.1 %all-reduce.11 = (f32[]{:T(128)}, f32[]{:T(128)}, f32[]{:T(128)}) all-reduce(f32[]{:T(128)S(6)} %mul.799, f32[]{:T(128)S(6)} %mul.806, f32[]{:T(128)S(6)} %mul.808), channel_id=1, replica_groups=mesh['row'=16,'col'=16] {'row'}, use_global_device_ids=true, to_apply=%region_92.93 | all-reduce | flops 3 | bytes 24 | tf_op jit(solution)/shard_map/psum | solution.py:122
  1378.6 36.1 %all-reduce.3 = (f32[]{:T(128)}, f32[]{:T(128)}, f32[]{:T(128)}) all-reduce(f32[]{:T(128)} %get-tuple-element.1831, f32[]{:T(128)} %get-tuple-element.1832, f32[]{:T(128)} %get-tuple-element.1833), channel_id=1, replica_groups=mesh['row'=16,'col'=16] {'col'}, use_global_device_ids=true, to_apply=%region_93.94 | all-reduce | flops 3 | bytes 24 | tf_op jit(solution)/shard_map/psum | solution.py:122
  1416.9 1.7 fusion.89
  1419.6 71.4 %psum.497 = f32[8192]{0:T(1024)S(1)} all-reduce(f32[8192]{0:T(1024)S(1)} %bitcast.332), channel_id=1, replica_groups=mesh['row'=16,'col'=16] {'col'}, use_global_device_ids=true, to_apply=%region_111.112 | all-reduce | flops 8192 | bytes 65536 | tf_op jit(solution)/shard_map/psum | solution.py:82
  1493.8 45.7 %psum.500 = f32[8192]{0:T(1024)S(1)} all-reduce(f32[8192]{0:T(1024)S(1)} %bitcast.333), channel_id=1, replica_groups=mesh['row'=16,'col'=16] {'row'}, use_global_device_ids=true, to_apply=%region_117.118 | all-reduce | flops 8192 | bytes 65536 | tf_op jit(solution)/shard_map/psum | solution.py:88
  1542.2 24.1 %all-reduce.10 = (f32[]{:T(128)}, f32[]{:T(128)}, f32[]{:T(128)}) all-reduce(f32[]{:T(128)S(6)} %mul.815, f32[]{:T(128)S(6)} %mul.822, f32[]{:T(128)S(6)} %mul.824), channel_id=1, replica_groups=mesh['row'=16,'col'=16] {'row'}, use_global_device_ids=true, to_apply=%region_107.108 | all-reduce | flops 3 | bytes 24 | tf_op jit(solution)/shard_map/psum | solution.py:122
  1566.4 36.1 %all-reduce.2 = (f32[]{:T(128)}, f32[]{:T(128)}, f32[]{:T(128)}) all-reduce(f32[]{:T(128)} %get-tuple-element.1828, f32[]{:T(128)} %get-tuple-element.1829, f32[]{:T(128)} %get-tuple-element.1830), channel_id=1, replica_groups=mesh['row'=16,'col'=16] {'col'}, use_global_device_ids=true, to_apply=%region_108.109 | all-reduce | flops 3 | bytes 24 | tf_op jit(solution)/shard_map/psum | solution.py:122
  1605.3 1.7 fusion.85
  1608.0 71.4 %psum.503 = f32[8192]{0:T(1024)S(1)} all-reduce(f32[8192]{0:T(1024)S(1)} %bitcast.317), channel_id=1, replica_groups=mesh['row'=16,'col'=16] {'col'}, use_global_device_ids=true, to_apply=%region_123.124 | all-reduce | flops 8192 | bytes 65536 | tf_op jit(solution)/shard_map/psum | solution.py:82
  (138 shorter events, 53.7 us)
Async XLA Ops:
  7.2 0.8 copy-start.1
  7.2 1.4 copy-start.2
  7.2 161.9 %copy-start = (f32[1,1,16,128,128]{4,3,2,1,0:T(8,128)S(1)}, f32[1,1,16,128,128]{4,3,2,1,0:T(8,128)}, u32[]{:S(2)}) copy-start(f32[1,1,16,128,128]{4,3,2,1,0:T(8,128)} %param.43) | copy-start | bytes 3145732
  7.2 1108.6 %all-reduce.19.cloned.1.call-start = ((), (), s32[]{:S(2)}) async-start(), calls=%async_computation | async-start | bytes 131072 | tf_op jit(solution)/shard_map/psum | solution.py:82
  91.7 76.6 %copy-start.3 = (f32[8192]{0:T(1024)S(1)}, f32[8192]{0:T(1024)}, u32[]{:S(2)}) copy-start(f32[8192]{0:T(1024)} %param.48) | copy-start | bytes 98308
  91.7 76.6 %copy-start.8 = (s32[8192]{0:T(1024)S(1)}, s32[8192]{0:T(1024)}, u32[]{:S(2)}) copy-start(s32[8192]{0:T(1024)} %param.49) | copy-start | bytes 98308
  168.3 0.7 copy-start.9
  170.9 0.7 copy-start.10
  172.5 70.9 %copy-start.7 = (s32[8192]{0:T(1024)S(1)}, s32[8192]{0:T(1024)}, u32[]{:S(2)}) copy-start(s32[8192]{0:T(1024)} %param.51) | copy-start | bytes 98308
  1025.2 1.7 copy-start.4
  1028.0 0.6 copy-start.5
  1233.5 69.8 %copy-start.6 = (f32[8192]{0:T(1024)S(1)}, f32[8192]{0:T(1024)}, u32[]{:S(2)}) copy-start(f32[8192]{0:T(1024)} %get-tuple-element.1815) | copy-start | bytes 98308
Sparse Core Ops, SparseCore 0:
  1028.8 87.0 all-reduce.18
